TPU v7x, 512 devices: a whole 4x4x16 slice. The times are simulated.
512 devices in a mesh: seq: 16 (over y, x), mp: 32 (over z, core).
Axes of the slice: x: 4, y: 4, z: 16, core: 2. Of those that a mesh axis runs over, the one named last changes fastest.
Arguments:
- q_proj: bfloat16 [4096, 8192], P('seq', 'mp'), may hold values from -6 to 6
- k_proj: bfloat16 [4096, 8192], P('seq', 'mp'), may hold values from -6 to 6
- v_proj: bfloat16 [4096, 8192], P('seq', 'mp'), may hold values from -6 to 6
- out_grad: bfloat16 [4096, 8192], P('seq', 'mp'), may hold values from -0.75 to 0.75
- out_weight: bfloat16 [8192, 8192], P('mp', 'seq'), may hold values from -0.0625 to 0.0625
- taps: float32 [7, 512], P(None, 'mp'), may hold values from -2.4 to 2.4
Outputs:
- grad_q: bfloat16 [4096, 8192], P('seq', 'mp')
- grad_k: bfloat16 [4096, 8192], P('seq', 'mp')
- grad_v: bfloat16 [4096, 8192], P('seq', 'mp')
- grad_weight: float32 [8192, 8192], P('mp', 'seq')
- grad_taps: float32 [7, 512], P(None, 'mp')
All inputs are finite; a program needn't handle non-finite values.
Results may differ from a plain program's by a relative error of at most 0.0029.
Values may be sent and summed in bfloat16 or wider, within the bound.
A program may use at most 64 MiB of HBM per device.

v0:
```python
import jax
import jax.numpy as jnp
from jax import lax
from jax.sharding import PartitionSpec as P

TAPS = 7
GROUP = 16


def passed_along(array, axis, by):
    count = lax.axis_size(axis)
    pairs = [(i, i + by) for i in range(count) if 0 <= i + by < count]
    return lax.ppermute(array, axis, pairs)


def shards(q_proj, k_proj, v_proj, out_grad, out_weight, taps):
    tokens, channels = q_proj.shape
    rim_rows = TAPS - 1
    q_full = q_proj.astype(jnp.float32)
    k_full = k_proj.astype(jnp.float32)
    v_full = v_proj.astype(jnp.float32)
    spread = jnp.broadcast_to(taps[:, :, None], (TAPS, taps.shape[1], GROUP)).reshape(
        TAPS, channels
    )
    tail_rows = jnp.stack([k_proj[tokens - rim_rows :], v_proj[tokens - rim_rows :]])
    before = passed_along(tail_rows, "seq", 1)
    keys_wide = jnp.concatenate([before[0], k_proj], 0).astype(jnp.float32)
    values_wide = jnp.concatenate([before[1], v_proj], 0).astype(jnp.float32)
    product = keys_wide * values_wide
    filtered = jnp.zeros((tokens, channels), jnp.float32)
    for offset in range(TAPS):
        filtered = (
            filtered + spread[offset] * product[rim_rows - offset : rim_rows - offset + tokens]
        )
    gated = (q_full * filtered).astype(jnp.bfloat16)
    seq_count, mp_count = (lax.axis_size("seq"), lax.axis_size("mp"))
    cores = mp_count // seq_count
    pairs = [
        (t * mp_count + cores * z + c, z * mp_count + cores * t + c)
        for t in range(seq_count)
        for z in range(seq_count)
        for c in range(cores)
    ]
    crossed = lax.ppermute(out_grad, ("seq", "mp"), pairs)
    tiles = lax.all_gather(crossed, "mp", axis=0)
    columns = (
        tiles.reshape(seq_count, cores, tokens, channels)
        .transpose(0, 2, 1, 3)
        .reshape(seq_count * tokens, cores * channels)
    )
    partial = lax.dot_general(
        columns, out_weight, (((1,), (1,)), ((), ())), preferred_element_type=jnp.float32
    )
    grad_gated = lax.psum_scatter(partial, "seq", scatter_dimension=0, tiled=True)
    grad_weight = lax.dot_general(
        lax.all_gather(gated, "seq", axis=0, tiled=True),
        columns,
        (((0,), (0,)), ((), ())),
        preferred_element_type=jnp.float32,
    )
    grad_q = (grad_gated * filtered).astype(jnp.bfloat16)
    grad_filtered = grad_gated * q_full
    following = passed_along(grad_filtered[:rim_rows], "seq", -1)
    grad_ext = jnp.concatenate([grad_filtered, following], 0)
    grad_product = jnp.zeros((tokens, channels), jnp.float32)
    for offset in range(TAPS):
        grad_product = grad_product + spread[offset] * grad_ext[offset : offset + tokens]
    grad_k = (grad_product * v_full).astype(jnp.bfloat16)
    grad_v = (grad_product * k_full).astype(jnp.bfloat16)
    filter_terms = jnp.stack(
        [
            jnp.sum(grad_filtered * product[rim_rows - offset : rim_rows - offset + tokens], 0)
            for offset in range(TAPS)
        ]
    )
    filter_local = filter_terms.reshape(TAPS, channels // GROUP, GROUP).sum(-1)
    grad_taps = lax.psum(filter_local, "seq")
    return (grad_q, grad_k, grad_v, grad_weight, grad_taps)


def solution(mesh):
    placed = (
        P("seq", "mp"),
        P("seq", "mp"),
        P("seq", "mp"),
        P("seq", "mp"),
        P("mp", "seq"),
        P(None, "mp"),
    )
    return jax.shard_map(
        shards,
        mesh=mesh,
        in_specs=placed,
        out_specs=(P("seq", "mp"), P("seq", "mp"), P("seq", "mp"), P("mp", "seq"), P(None, "mp")),
        check_vma=False,
    )
```

profile of v0, /device:TPU:32, one launch (start us, length us, event | category | flops | bytes accessed | tf_op | source)
XLA Modules:
  0.0 327.7 jit_solution(6569584320959466278)
XLA Ops:
  7.2 3.1 collective-permute-start
  10.3 12.5 %collective-permute-done = bf16[256,256]{1,0:T(8,128)(2,1)S(1)} collective-permute-done((bf16[256,256]{1,0:T(8,128)(2,1)}, bf16[256,256]{1,0:T(8,128)(2,1)S(1)}, u32[]{:S(2)}, u32[]{:S(2)}) %collective-permute-start) | collective-permute-done | bytes 131104 | tf_op jit(solution)/shard_map/ppermute | solution.py:44
  22.8 0.7 copy-done.5
  23.5 0.7 slice_bitcast_fusion.2
  24.3 1.3 collective-permute-start.1
  25.6 0.9 slice_bitcast_fusion.10
  26.6 0.1 broadcast_in_dim.45
  26.8 0.1 broadcast_in_dim.43
  26.9 0.1 broadcast_in_dim.41
  27.1 0.1 broadcast_in_dim.39
  27.2 0.1 broadcast_in_dim.37
  27.4 0.1 broadcast_in_dim.35
  27.5 0.1 broadcast_in_dim.33
  27.6 1.0 convert_multiply_fusion.2
  28.7 1.8 fusion
  30.6 87.3 %all-gather.6.cloned.1.call-done = bf16[8192,256]{1,0:T(8,128)(2,1)} async-done(((bf16[256,256]{1,0:T(8,128)(2,1)}), bf16[8192,256]{1,0:T(8,128)(2,1)}) %all-gather.6.cloned.1.call-update) | async-done | bytes 4194320 | tf_op jit(solution)/shard_map/all_gather | solution.py:45
  117.8 8.0 %copy.12 = bf16[16,2,256,256]{2,0,3,1:T(8,128)(2,1)} copy(bf16[16,2,256,256]{3,2,1,0:T(8,128)(2,1)} %bitcast.36) | data formatting | bytes 8388608 | tf_op jit(solution)/shard_map/reshape | solution.py:47
  125.8 4.4 %copy.13 = bf16[64,8,16,256]{3,1,2,0:T(8,128)(2,1)S(1)} copy(bf16[64,8,16,256]{3,2,1,0:T(8,128)(2,1)} %bitcast.35) | data formatting | bytes 8388608
  130.2 2.0 copy-done.1
  132.2 3.2 fusion.19
  135.5 43.0 %all-gather.4.cloned.1.call-done = bf16[4096,256]{1,0:T(8,128)(2,1)} async-done(((bf16[256,256]{1,0:T(8,128)(2,1)}), bf16[4096,256]{1,0:T(8,128)(2,1)}) %all-gather.4.cloned.1.call-update) | async-done | bytes 2097168 | tf_op jit(solution)/shard_map/all_gather | solution.py:56
  178.5 4.9 %fusion.20 = f32[256,512]{1,0:T(8,128)} fusion(bf16[4096,256]{1,0:T(8,128)(2,1)} %all-gather.4.cloned.1.call-done, bf16[4096,512]{0,1:T(8,128)(2,1)} %bitcast.34), kind=kOutput, calls=%fused_computation.61 | convolution fusion | flops 1073741824 | bytes 6815744 | tf_op jit(solution)/shard_map/dot_general | solution.py:55
  183.4 91.8 %reduce-scatter.2.cloned.1.call-done = f32[256,256]{1,0:T(8,128)} async-done(((f32[4096,256]{1,0:T(8,128)}), f32[256,256]{1,0:T(8,128)}) %reduce-scatter.2.cloned.1.call-update) | async-done | bytes 262160 | tf_op jit(solution)/shard_map/reduce_scatter | solution.py:54
  275.2 1.9 multiply_reduce_fusion
  277.1 1.3 collective-permute-start.2
  278.4 0.1 stack.36
  278.4 0.1 stack.37
  278.5 0.1 stack.38
  279.0 0.1 reduce_sum.79
  279.1 40.5 %psum.7 = f32[7,16]{1,0:T(8,128)} all-reduce(f32[7,16]{1,0:T(8,128)S(1)} %reduce_sum.79), channel_id=1, replica_groups=mesh['seq'=16,'mp'=32] {'seq'}, use_global_device_ids=true, to_apply=%region_9.0 | all-reduce | flops 112 | bytes 896 | tf_op jit(solution)/shard_map/psum | solution.py:77
  319.6 0.9 multiply_convert_fusion
  320.5 0.7 multiply_convert_fusion.1
  (39 shorter events, 1.1 us)
Async XLA Ops:
  7.2 125.0 %copy-start = (bf16[256,512]{1,0:T(8,128)(2,1)S(1)}, bf16[256,512]{1,0:T(8,128)(2,1)}, u32[]{:S(2)}) copy-start(bf16[256,512]{1,0:T(8,128)(2,1)} %param.10) | copy-start | bytes 786436
  7.2 110.7 %all-gather.6.cloned.1.call-start = ((), (), s32[]{:S(2)}) async-start(), calls=%async_computation.3 | async-start | bytes 4325376 | tf_op jit(solution)/shard_map/all_gather | solution.py:45
  7.2 15.6 %collective-permute-start = (bf16[256,256]{1,0:T(8,128)(2,1)}, bf16[256,256]{1,0:T(8,128)(2,1)S(1)}, u32[]{:S(2)}, u32[]{:S(2)}) collective-permute-start(bf16[256,256]{1,0:T(8,128)(2,1)} %param.9), channel_id=1, source_target_pairs={{0,0},{1,1},{2,32},{3,33},{4,64},{5,65},{6,96},{7,97},{8,128},{9,1... | collective-permute-start | bytes 393224 | tf_op jit(solution)/shard_map/ppermute | solution.py:44
  22.8 0.7 copy-start.5
  23.5 155.0 %all-gather.4.cloned.1.call-start = ((), (), s32[]{:S(2)}) async-start(), calls=%async_computation.2 | async-start | bytes 2228224 | tf_op jit(solution)/shard_map/all_gather | solution.py:56
  24.3 3.3 %collective-permute-start.1 = (bf16[2,6,256]{2,1,0:T(8,128)(2,1)S(1)}, bf16[2,6,256]{2,1,0:T(8,128)(2,1)S(1)}, u32[]{:S(2)}, u32[]{:S(2)}) collective-permute-start(bf16[2,6,256]{2,1,0:T(8,128)(2,1)S(1)} %pad_maximum_fusion.1), channel_id=1, source_target_pairs={{0,32},{32,64},{64,96},{96,128},{128,160},{160,192},{192,224},{224... | collective-permute-start | bytes 18440 | tf_op jit(solution)/shard_map/ppermute | solution.py:13
  30.5 244.7 %reduce-scatter.2.cloned.1.call-start = ((), (), s32[]{:S(2)}) async-start(), calls=%async_computation.1 | async-start | bytes 4456448 | tf_op jit(solution)/shard_map/reduce_scatter | solution.py:54
  130.2 2.0 copy-start.1
  135.4 139.8 %copy-start.4 = (bf16[256,256]{1,0:T(8,128)(2,1)S(1)}, bf16[256,256]{1,0:T(8,128)(2,1)}, u32[]{:S(2)}) copy-start(bf16[256,256]{1,0:T(8,128)(2,1)} %param.6) | copy-start | bytes 393220
  135.4 184.1 %copy-start.2 = (bf16[256,256]{1,0:T(8,128)(2,1)S(1)}, bf16[256,256]{1,0:T(8,128)(2,1)}, u32[]{:S(2)}) copy-start(bf16[256,256]{1,0:T(8,128)(2,1)} %param.7) | copy-start | bytes 393220
  135.4 185.0 %copy-start.3 = (bf16[256,256]{1,0:T(8,128)(2,1)S(1)}, bf16[256,256]{1,0:T(8,128)(2,1)}, u32[]{:S(2)}) copy-start(bf16[256,256]{1,0:T(8,128)(2,1)} %param.8) | copy-start | bytes 393220
  277.1 42.5 %collective-permute-start.2 = (f32[6,256]{1,0:T(8,128)S(1)}, f32[6,256]{1,0:T(8,128)S(1)}, u32[]{:S(2)}, u32[]{:S(2)}) collective-permute-start(f32[6,256]{1,0:T(8,128)S(1)} %slice.158), channel_id=1, source_target_pairs={{32,0},{64,32},{96,64},{128,96},{160,128},{192,160},{224,192},{256... | collective-permute-start | bytes 18440 | tf_op jit(solution)/shard_map/ppermute | solution.py:13
Sparse Core Ops, SparseCore 0:
  23.6 94.1 all-gather.5
  121.4 57.0 all-gather.3
  182.7 92.4 reduce-scatter.1
where the time goes:
time: 328 us
  waiting for transfers between devices  235 us (72%)
  blocking collectives  40.5 us (12%)
  local copies, waits for them, and re-layouts  18.3 us (6%)
  between operations  13.9 us (4%)
  matrix products  8.15 us (2%)
  other arithmetic  6.39 us (2%)
  starting transfers between devices  5.76 us (2%)
    reduce_scatter x1, waiting for transfers between devices, shards(): lax.psum_scatter(partial, 'seq', scatter_dimension=0, tiled=True)  91.8 us
    all_gather x1, waiting for transfers between devices, shards(): tiles = lax.all_gather(crossed, 'mp', axis=0)  87.3 us
    all_gather x1, waiting for transfers between devices, shards(): lax.all_gather(gated, 'seq', axis=0, tiled=True)  43 us
    psum x1, blocking collectives, shards(): grad_taps = lax.psum(filter_local, 'seq')  40.5 us
    ppermute x1, waiting for transfers between devices, shards(): crossed = lax.ppermute(out_grad, ('seq', 'mp'), pairs)  12.5 us
    reshape x1, local copies, waits for them, and re-layouts, shards(): tiles.reshape(seq_count, cores, tokens, channels).transpose(0, 2, 1, 3)  7.96 us
    unnamed x19, local copies, waits for them, and re-layouts  7.08 us
  transfers between devices with their start and end apart: 6, of which 4 were waited for; matrix products, arithmetic and copies ran while one was open for 8% of the time, Pallas kernels for 0%

commit v1 on v0

--- a/solution.py
+++ b/solution.py
@@ -52,8 +52,17 @@
         columns, out_weight, (((1,), (1,)), ((), ())), preferred_element_type=jnp.float32
     )
     grad_gated = lax.psum_scatter(partial, "seq", scatter_dimension=0, tiled=True)
+    handle_space = lambda page, which_axis: jnp.concatenate(
+        jax.lax.all_to_all(
+            jnp.stack([page] * jax.lax.axis_size(which_axis)),
+            which_axis,
+            split_axis=0,
+            concat_axis=0,
+        ),
+        axis=0,
+    )
     grad_weight = lax.dot_general(
-        lax.all_gather(gated, "seq", axis=0, tiled=True),
+        handle_space(gated, "seq"),
         columns,
         (((0,), (0,)), ((), ())),
         preferred_element_type=jnp.float32,

time: 328 us -> 291 us (0.89)
  waiting for transfers between devices: 235 us -> 159 us
  blocking collectives: 40.5 us -> 82 us
    all_gather x1 -> x0, waiting for transfers between devices: 43 us -> none  [shards(): lax.all_gather(gated, 'seq', axis=0, tiled=True)]
    all_to_all x0 -> x1, blocking collectives: none -> 41.5 us  [shards(): jax.lax.all_to_all(jnp.stack([page] * jax.lax.axis_size(which_axis)), whi...]
    reduce_scatter x1, waiting for transfers between devices: 91.8 us -> 52.4 us  [shards(): lax.psum_scatter(partial, 'seq', scatter_dimension=0, tiled=True)]
    all_gather x1, waiting for transfers between devices: 87.3 us -> 94.4 us  [shards(): tiles = lax.all_gather(crossed, 'mp', axis=0)]
    unnamed x19 -> x23, local copies, waits for them, and re-layouts: 7.08 us -> 8.01 us
  transfers between devices with their start and end apart: 6 -> 5, of which waited for: 4 -> 4; matrix products, arithmetic and copies ran while one was open for 8% -> 2% of each run, Pallas kernels for 0% -> 0%
where the time goes in v1:
time: 291 us; the launch traced here: 290 us
  waiting for transfers between devices  159 us (55%)
  blocking collectives  82 us (28%)
  local copies, waits for them, and re-layouts  17.8 us (6%)
  between operations  14.2 us (5%)
  starting transfers between devices  7.7 us (3%)
  matrix products  5.32 us (2%)
  other arithmetic  3.87 us (1%)
    all_gather x1, waiting for transfers between devices, shards(): tiles = lax.all_gather(crossed, 'mp', axis=0)  94.4 us
    reduce_scatter x1, waiting for transfers between devices, shards(): lax.psum_scatter(partial, 'seq', scatter_dimension=0, tiled=True)  52.4 us
    all_to_all x1, blocking collectives, shards(): jax.lax.all_to_all(jnp.stack([page] * jax.lax.axis_size(which_axis)), whi...  41.5 us
    psum x1, blocking collectives, shards(): grad_taps = lax.psum(filter_local, 'seq')  40.5 us
    ppermute x1, waiting for transfers between devices, shards(): crossed = lax.ppermute(out_grad, ('seq', 'mp'), pairs)  12.4 us
    unnamed x23, local copies, waits for them, and re-layouts  8.01 us
    reshape x1, local copies, waits for them, and re-layouts, shards(): tiles.reshape(seq_count, cores, tokens, channels).transpose(0, 2, 1, 3)  7.96 us
  transfers between devices with their start and end apart: 5, of which 4 were waited for; matrix products, arithmetic and copies ran while one was open for 2% of the time, Pallas kernels for 0%

profile of v1, /device:TPU:32, one launch (start us, length us, event | category | flops | bytes accessed | tf_op | source)
XLA Modules:
  0.0 290.3 jit_solution(15166342369340379769)
XLA Ops:
  7.2 3.1 %collective-permute-start = (bf16[256,256]{1,0:T(8,128)(2,1)}, bf16[256,256]{1,0:T(8,128)(2,1)S(1)}, u32[]{:S(2)}, u32[]{:S(2)}) collective-permute-start(bf16[256,256]{1,0:T(8,128)(2,1)} %param.9), channel_id=1, source_target_pairs={{0,0},{1,1},{2,32},{3,33},{4,64},{5,65},{6,96},{7,97},{8,128},{9,1... | collective-permute-start | bytes 393224 | tf_op jit(solution)/shard_map/ppermute | solution.py:44
  10.3 12.4 %collective-permute-done = bf16[256,256]{1,0:T(8,128)(2,1)S(1)} collective-permute-done((bf16[256,256]{1,0:T(8,128)(2,1)}, bf16[256,256]{1,0:T(8,128)(2,1)S(1)}, u32[]{:S(2)}, u32[]{:S(2)}) %collective-permute-start) | collective-permute-done | bytes 131104 | tf_op jit(solution)/shard_map/ppermute | solution.py:44
  22.7 0.7 copy-done.6
  23.4 94.4 %all-gather.3.cloned.1.call-done = bf16[8192,256]{1,0:T(8,128)(2,1)} async-done(((bf16[256,256]{1,0:T(8,128)(2,1)}), bf16[8192,256]{1,0:T(8,128)(2,1)}) %all-gather.3.cloned.1.call-update) | async-done | bytes 4194320 | tf_op jit(solution)/shard_map/all_gather | solution.py:45
  117.9 8.0 %copy.12 = bf16[16,2,256,256]{2,0,3,1:T(8,128)(2,1)} copy(bf16[16,2,256,256]{3,2,1,0:T(8,128)(2,1)} %bitcast.37) | data formatting | bytes 8388608 | tf_op jit(solution)/shard_map/reshape | solution.py:47
  125.8 4.4 %copy.13 = bf16[64,8,16,256]{3,1,2,0:T(8,128)(2,1)S(1)} copy(bf16[64,8,16,256]{3,2,1,0:T(8,128)(2,1)} %bitcast.36) | data formatting | bytes 8388608
  130.2 2.0 copy-done.1
  132.2 3.2 %fusion.19 = f32[4096,256]{1,0:T(8,128)} fusion(bf16[4096,512]{0,1:T(8,128)(2,1)S(1)} %bitcast.34, bf16[256,512]{1,0:T(8,128)(2,1)S(1)} %copy-done), kind=kOutput, calls=%fused_computation.60 | convolution fusion | flops 1073741824 | bytes 8650752 | tf_op jit(solution)/shard_map/dot_general | solution.py:51
  135.5 0.9 copy-done.3
  136.4 3.3 %collective-permute-start.1 = (bf16[2,6,256]{2,1,0:T(8,128)(2,1)S(1)}, bf16[2,6,256]{2,1,0:T(8,128)(2,1)S(1)}, u32[]{:S(2)}, u32[]{:S(2)}) collective-permute-start(bf16[2,6,256]{2,1,0:T(8,128)(2,1)S(1)} %pad_maximum_fusion.1), channel_id=1, source_target_pairs={{0,32},{32,64},{64,96},{96,128},{128,160},{160,192},{192,224},{224... | collective-permute-start | bytes 18440 | tf_op jit(solution)/shard_map/ppermute | solution.py:13
  139.8 0.1 broadcast_in_dim.45
  139.9 0.1 broadcast_in_dim.43
  140.1 0.1 broadcast_in_dim.41
  140.2 0.1 broadcast_in_dim.39
  140.4 0.1 broadcast_in_dim.37
  140.5 0.1 broadcast_in_dim.35
  140.7 0.1 broadcast_in_dim.33
  140.8 0.3 collective-permute-done.1
  141.1 0.2 fusion
  141.4 0.2 stack.27
  141.6 41.5 %all_to_all.5 = bf16[16,256,256]{2,1,0:T(8,128)(2,1)S(1)} all-to-all(bf16[16,256,256]{2,1,0:T(8,128)(2,1)S(1)} %stack.27), channel_id=1, replica_groups=mesh['seq'=16,'mp'=32] {'seq'}, dimensions={0} | all-to-all | bytes 4194304 | tf_op jit(solution)/shard_map/all_to_all | solution.py:56
  183.1 2.1 fusion.20
  185.2 52.4 %reduce-scatter.2.cloned.1.call-done = f32[256,256]{1,0:T(8,128)} async-done(((f32[4096,256]{1,0:T(8,128)}), f32[256,256]{1,0:T(8,128)}) %reduce-scatter.2.cloned.1.call-update) | async-done | bytes 262160 | tf_op jit(solution)/shard_map/reduce_scatter | solution.py:54
  237.5 1.9 multiply_reduce_fusion
  239.4 1.3 collective-permute-start.2
  240.7 0.1 stack.56
  240.8 0.1 stack.57
  241.0 0.1 stack.60
  241.3 0.1 reduce_sum.79
  241.4 40.5 %psum.7 = f32[7,16]{1,0:T(8,128)} all-reduce(f32[7,16]{1,0:T(8,128)S(1)} %reduce_sum.79), channel_id=1, replica_groups=mesh['seq'=16,'mp'=32] {'seq'}, use_global_device_ids=true, to_apply=%region_9.0 | all-reduce | flops 112 | bytes 896 | tf_op jit(solution)/shard_map/psum | solution.py:86
  281.9 0.9 multiply_convert_fusion
  282.8 0.7 multiply_convert_fusion.1
  (42 shorter events, 1.1 us)
Async XLA Ops:
  7.2 125.0 %copy-start = (bf16[256,512]{1,0:T(8,128)(2,1)S(1)}, bf16[256,512]{1,0:T(8,128)(2,1)}, u32[]{:S(2)}) copy-start(bf16[256,512]{1,0:T(8,128)(2,1)} %param.10) | copy-start | bytes 786436
  7.2 110.7 %all-gather.3.cloned.1.call-start = ((), (), s32[]{:S(2)}) async-start(), calls=%async_computation.3 | async-start | bytes 4325376 | tf_op jit(solution)/shard_map/all_gather | solution.py:45
  7.2 15.5 %collective-permute-start = (bf16[256,256]{1,0:T(8,128)(2,1)}, bf16[256,256]{1,0:T(8,128)(2,1)S(1)}, u32[]{:S(2)}, u32[]{:S(2)}) collective-permute-start(bf16[256,256]{1,0:T(8,128)(2,1)} %param.9), channel_id=1, source_target_pairs={{0,0},{1,1},{2,32},{3,33},{4,64},{5,65},{6,96},{7,97},{8,128},{9,1... | collective-permute-start | bytes 393224 | tf_op jit(solution)/shard_map/ppermute | solution.py:44
  22.7 0.7 copy-start.6
  23.4 214.1 %reduce-scatter.2.cloned.1.call-start = ((), (), s32[]{:S(2)}) async-start(), calls=%async_computation.2 | async-start | bytes 4456448 | tf_op jit(solution)/shard_map/reduce_scatter | solution.py:54
  130.2 2.0 copy-start.1
  135.4 0.9 copy-start.3
  135.4 1.0 copy-start.4
  135.4 4.3 %copy-start.7 = (f32[7,16]{1,0:T(8,128)S(1)}, f32[7,16]{1,0:T(8,128)}, u32[]{:S(2)}) copy-start(f32[7,16]{1,0:T(8,128)} %param.11) | copy-start | bytes 1348
  135.4 5.7 %copy-start.5 = (bf16[256,256]{1,0:T(8,128)(2,1)S(1)}, bf16[256,256]{1,0:T(8,128)(2,1)}, u32[]{:S(2)}) copy-start(bf16[256,256]{1,0:T(8,128)(2,1)} %param.6) | copy-start | bytes 393220
  136.4 4.6 %collective-permute-start.1 = (bf16[2,6,256]{2,1,0:T(8,128)(2,1)S(1)}, bf16[2,6,256]{2,1,0:T(8,128)(2,1)S(1)}, u32[]{:S(2)}, u32[]{:S(2)}) collective-permute-start(bf16[2,6,256]{2,1,0:T(8,128)(2,1)S(1)} %pad_maximum_fusion.1), channel_id=1, source_target_pairs={{0,32},{32,64},{64,96},{96,128},{128,160},{160,192},{192,224},{224... | collective-permute-start | bytes 18440 | tf_op jit(solution)/shard_map/ppermute | solution.py:13
  141.1 41.9 %copy-start.2 = (bf16[64,8,16,256]{3,1,2,0:T(8,128)(2,1)S(1)}, bf16[64,8,16,256]{3,1,2,0:T(8,128)(2,1)}, u32[]{:S(2)}) copy-start(bf16[64,8,16,256]{3,1,2,0:T(8,128)(2,1)} %copy-done.1) | copy-start | bytes 12582916
  239.4 42.5 %collective-permute-start.2 = (f32[6,256]{1,0:T(8,128)S(1)}, f32[6,256]{1,0:T(8,128)S(1)}, u32[]{:S(2)}, u32[]{:S(2)}) collective-permute-start(f32[6,256]{1,0:T(8,128)S(1)} %slice.158), channel_id=1, source_target_pairs={{32,0},{64,32},{96,64},{128,96},{160,128},{192,160},{224,192},{256... | collective-permute-start | bytes 18440 | tf_op jit(solution)/shard_map/ppermute | solution.py:13
Sparse Core Ops, SparseCore 0:
  23.5 94.3 all-gather.2
  135.6 101.8 reduce-scatter.1
